TPU v7x, 512 devices: a whole 4x4x16 slice. The times are simulated.
512 devices in a mesh: chan: 32 (over y, z_lo), ctx: 16 (over z_hi, x, core).
Axes of the slice: x: 4, y: 4, z: 16 (z_hi: 2, z_lo: 8; z = z_hi * 8 + z_lo), core: 2. Of those that a mesh axis runs over, the one named last changes fastest.
Arguments:
- inputs: bfloat16 [2048, 8192], P('ctx', 'chan'), may hold values from -6 to 6
- gate: bfloat16 [2048, 8192], P('ctx', 'chan'), may hold values from -200 to 200
- filter_taps: bfloat16 [2048, 8192], P('ctx', 'chan'), may hold values from -4 to 4, as said below
- cotangent: bfloat16 [2048, 8192], P('ctx', 'chan'), may hold values from -6 to 6
Outputs:
- output: bfloat16 [2048, 8192], P('ctx', 'chan')
- gate_grad: bfloat16 [2048, 8192], P('ctx', 'chan')
- input_grad: bfloat16 [2048, 8192], P('ctx', 'chan')
- filter_grad: float32 [2048, 8192], P('ctx', 'chan')
Inputs may be any that keep to these rules, and one draw needn't show every extreme that they name: `filter_taps`: each channel's filter taps shrink with the lag at a rate of their own.
All inputs are finite; a program needn't handle non-finite values.
Results may differ from a plain program's by a relative error of at most 0.005.
Values may be sent and summed in bfloat16 or wider, within the bound.
A program may use at most 64 MiB of HBM per device.

v0:
```python
import math
import jax
import jax.numpy as jnp
from jax import lax
from jax.sharding import PartitionSpec as P

HIGHEST = lax.Precision.HIGHEST
EPSILON = 1e-06


def tables(block_len):
    period = 2 * block_len
    offsets = jnp.arange(block_len, dtype=jnp.int32)
    harmonics = jnp.arange(block_len + 1, dtype=jnp.int32)
    samples = jnp.arange(period, dtype=jnp.int32)
    radians = math.pi / block_len
    angles = jnp.mod(harmonics[:, None] * offsets[None, :], period).astype(jnp.float32) * radians
    back_angles = (
        jnp.mod(samples[:, None] * harmonics[None, :], period).astype(jnp.float32) * radians
    )
    weights = (
        jnp.where((harmonics == 0) | (harmonics == block_len), 1.0, 2.0).astype(jnp.float32)
        / period
    )
    return (
        jnp.cos(angles),
        jnp.sin(angles),
        jnp.cos(back_angles) * weights[None, :],
        jnp.sin(back_angles) * weights[None, :],
    )


def spectrum(series, block_len, fwd_cos, fwd_sin):
    number = series.shape[0] // block_len
    blocks = series.astype(jnp.float32).reshape(number, block_len, series.shape[1])
    real_part = jnp.einsum("kn,bnc->bkc", fwd_cos, blocks, precision=HIGHEST)
    imag_part = -jnp.einsum("kn,bnc->bkc", fwd_sin, blocks, precision=HIGHEST)
    return (real_part, imag_part)


def inverse_many(real_part, imag_part, inv_cos, inv_sin):
    return jnp.einsum("mk,skc->smc", inv_cos, real_part, precision=HIGHEST) - jnp.einsum(
        "mk,skc->smc", inv_sin, imag_part, precision=HIGHEST
    )


def select(spectra, position):
    number = spectra[0].shape[0]
    inside = jnp.logical_and(position >= 0, position < number)
    clipped = jnp.clip(position, 0, number - 1)
    real_part = lax.dynamic_index_in_dim(spectra[0], clipped, 0, keepdims=False)
    imag_part = lax.dynamic_index_in_dim(spectra[1], clipped, 0, keepdims=False)
    return (jnp.where(inside, real_part, 0.0), jnp.where(inside, imag_part, 0.0))


def product(left, right, conjugate):
    if conjugate:
        return (left[0] * right[0] + left[1] * right[1], left[0] * right[1] - left[1] * right[0])
    return (left[0] * right[0] - left[1] * right[1], left[0] * right[1] + left[1] * right[0])


def forward_terms(taps_spec, input_spec, first_block, targets):
    empty = jnp.zeros((targets,) + taps_spec[0].shape[1:], jnp.float32)

    def forward_advance(offset, totals):
        reals, imags = totals
        kernel = select(taps_spec, offset)
        for target in range(targets):
            addend = product(kernel, select(input_spec, first_block - 1 + target - offset), False)
            reals = reals.at[target].add(addend[0])
            imags = imags.at[target].add(addend[1])
        return (reals, imags)

    return lax.fori_loop(0, taps_spec[0].shape[0], forward_advance, (empty, empty))


def backward_terms(taps_spec, inner_spec, first_block, targets):
    empty = jnp.zeros((targets,) + taps_spec[0].shape[1:], jnp.float32)

    def backward_advance(offset, totals):
        reals, imags = totals
        kernel = select(taps_spec, offset)
        for target in range(targets):
            addend = product(kernel, select(inner_spec, first_block + target + offset), True)
            reals = reals.at[target].add(addend[0])
            imags = imags.at[target].add(addend[1])
        return (reals, imags)

    return lax.fori_loop(0, taps_spec[0].shape[0], backward_advance, (empty, empty))


def owner_terms(input_spec, inner_spec, first_block, targets):
    empty = jnp.zeros((targets,) + input_spec[0].shape[1:], jnp.float32)

    def owner_advance(later, totals):
        reals, imags = totals
        grads = select(inner_spec, later)
        for target in range(targets):
            addend = product(select(input_spec, later - first_block - target), grads, True)
            reals = reals.at[target].add(addend[0])
            imags = imags.at[target].add(addend[1])
        return (reals, imags)

    return lax.fori_loop(0, input_spec[0].shape[0], owner_advance, (empty, empty))


def local(inputs, gate, filter_taps, cotangent):
    row_count, local_chan = inputs.shape
    block_len = min(128, row_count)
    slot_count = row_count // block_len
    first_block = lax.axis_index("ctx") * slot_count
    seq_total = row_count * lax.axis_size("ctx")
    fwd_cos, fwd_sin, inv_cos, inv_sin = tables(block_len)
    all_taps = lax.all_gather(filter_taps, "ctx", axis=0, tiled=True)
    taps_spec = spectrum(all_taps, block_len, fwd_cos, fwd_sin)
    all_inputs = lax.all_gather(inputs, "ctx", axis=0, tiled=True)
    input_spec = spectrum(all_inputs, block_len, fwd_cos, fwd_sin)
    conv_real, conv_imag = forward_terms(taps_spec, input_spec, first_block, slot_count + 1)
    waves = inverse_many(conv_real, conv_imag, inv_cos, inv_sin)
    convolved = (waves[1:, :block_len] + waves[:-1, block_len:]).reshape(row_count, local_chan)
    gate_wide = gate.astype(jnp.float32)
    upstream = cotangent.astype(jnp.float32)
    mixed = gate_wide * convolved
    squares, projection = lax.psum(
        (jnp.sum(mixed * mixed, axis=1), jnp.sum(upstream * mixed, axis=1)), "chan"
    )
    channels = local_chan * lax.axis_size("chan")
    inv_rms = lax.rsqrt(squares / channels + EPSILON)[:, None]
    output = (mixed * inv_rms).astype(jnp.bfloat16)
    d_mixed = inv_rms * upstream - mixed * inv_rms**3 * projection[:, None] / channels
    gate_grad = (d_mixed * convolved).astype(jnp.bfloat16)
    d_inner = (d_mixed * gate_wide).astype(jnp.bfloat16)
    all_inner = lax.all_gather(d_inner, "ctx", axis=0, tiled=True)
    inner_spec = spectrum(all_inner, block_len, fwd_cos, fwd_sin)
    back_real, back_imag = backward_terms(taps_spec, inner_spec, first_block, slot_count + 1)
    waves = inverse_many(back_real, back_imag, inv_cos, inv_sin)
    input_grad = (
        (waves[:-1, :block_len] + waves[1:, block_len:])
        .reshape(row_count, local_chan)
        .astype(jnp.bfloat16)
    )
    lag_real, lag_imag = owner_terms(input_spec, inner_spec, first_block, slot_count + 1)
    waves = inverse_many(lag_real, lag_imag, inv_cos, inv_sin)
    filter_sum = (waves[:-1, :block_len] + waves[1:, block_len:]).reshape(row_count, local_chan)
    filter_grad = filter_sum / math.sqrt(seq_total)
    return (output, gate_grad, input_grad, filter_grad)


def solution(mesh):
    in_specs = (P("ctx", "chan"), P("ctx", "chan"), P("ctx", "chan"), P("ctx", "chan"))
    out_specs = (P("ctx", "chan"), P("ctx", "chan"), P("ctx", "chan"), P("ctx", "chan"))
    return jax.shard_map(local, mesh=mesh, in_specs=in_specs, out_specs=out_specs, check_vma=False)
```

profile of v0, /device:TPU:1, one launch (start us, length us, event | category | flops | bytes accessed | tf_op | source)
XLA Modules:
  0.0 500.6 jit_solution(9985710225990442809)
XLA Ops:
  10.6 84.2 %all-gather.6.cloned.1.call-done = bf16[2048,256]{1,0:T(8,128)(2,1)} async-done(((bf16[128,256]{1,0:T(8,128)(2,1)}), bf16[2048,256]{1,0:T(8,128)(2,1)}) %all-gather.6.cloned.1.call-update) | async-done | bytes 1048592 | tf_op jit(solution)/shard_map/all_gather | solution.py:116
  94.8 4.0 convolution_bitcast_fusion.1
  98.8 2.6 negate_bitcast_fusion.1
  101.5 65.2 %all-gather.4.cloned.1.call-done = bf16[2048,256]{1,0:T(8,128)(2,1)} async-done(((bf16[128,256]{1,0:T(8,128)(2,1)}), bf16[2048,256]{1,0:T(8,128)(2,1)}) %all-gather.4.cloned.1.call-update) | async-done | bytes 1048592 | tf_op jit(solution)/shard_map/all_gather | solution.py:114
  166.7 2.6 convolution_bitcast_fusion.2
  169.3 2.6 negate_bitcast_fusion.2
  172.0 38.1 %while.63 = (s32[]{:T(128)}, f32[2,129,256]{2,1,0:T(8,128)S(1)}, f32[2,129,256]{2,1,0:T(8,128)S(1)}, f32[16,129,256]{2,1,0:T(8,128)S(1)}, s32[]{:T(128)}, /*inde...) while((s32[]{:T(128)}, f32[2,129,256]{2,1,0:T(8,128)S(1)}, ...), condition=%wide.region_1.2_spmd, body=%wide.region_0.1_spmd.sunk | while | flops 792593 | bytes 2185508 | solution.py:74
  210.1 1.4 fusion.19
  211.5 1.5 fusion.8
  213.0 102.0 %all-reduce = (f32[128]{0:T(128)S(1)}, f32[128]{0:T(128)S(1)}) all-reduce(f32[128]{0:T(128)S(1)} %get-tuple-element.897, f32[128]{0:T(128)S(1)} %get-tuple-element.896), channel_id=1, replica_groups=mesh['chan'=32,'ctx'=16] {'chan'}, use_global_device_ids=true, to_apply=%region_3.4 | all-reduce | flops 256 | bytes 2048 | tf_op jit(solution)/shard_map/psum | solution.py:124
  317.3 84.4 %all-gather.8.cloned.1.call-done = bf16[2048,256]{0,1:T(8,128)(2,1)} async-done(((bf16[128,256]{0,1:T(8,128)(2,1)}), bf16[2048,256]{0,1:T(8,128)(2,1)}) %all-gather.8.cloned.1.call-update) | async-done | bytes 1048592 | tf_op jit(solution)/shard_map/all_gather | solution.py:133
  401.7 1.5 copy.16
  403.2 2.6 convolution_bitcast_fusion
  405.8 2.7 negate_bitcast_fusion
  408.6 40.0 %while.65 = (s32[]{:T(128)}, f32[2,129,256]{2,1,0:T(8,128)S(1)}, f32[2,129,256]{2,1,0:T(8,128)S(1)}, s32[]{:T(128)}, f32[16,129,256]{2,1,0:T(8,128)}, /*index=5*...) while((s32[]{:T(128)}, f32[2,129,256]{2,1,0:T(8,128)S(1)}, ...), condition=%wide.region_9.10_spmd, body=%wide.region_8.9_spmd.sunk | while | flops 792593 | bytes 2171172 | solution.py:104
  409.8 1.2 fusion.131
  414.8 1.2 fusion.131
  417.3 1.2 fusion.131
  419.8 1.2 fusion.131
  448.6 1.4 fusion.15
  450.0 1.5 fusion.6
  452.3 38.1 %while.64 = (s32[]{:T(128)}, f32[2,129,256]{2,1,0:T(8,128)S(1)}, f32[2,129,256]{2,1,0:T(8,128)S(1)}, f32[16,129,256]{2,1,0:T(8,128)S(1)}, s32[]{:T(128)}, /*inde...) while((s32[]{:T(128)}, f32[2,129,256]{2,1,0:T(8,128)S(1)}, ...), condition=%wide.region_7.8_spmd, body=%wide.region_6.7_spmd.sunk | while | flops 792593 | bytes 2185508 | solution.py:89
  490.4 1.4 fusion.17
  491.8 1.5 fusion.7
  (120 shorter events, 116.1 us)
Async XLA Ops:
  7.2 87.7 %all-gather.6.cloned.1.call-start = ((), (), s32[]{:S(2)}) async-start(), calls=%async_computation.1 | async-start | bytes 1114112 | tf_op jit(solution)/shard_map/all_gather | solution.py:116
  7.9 158.8 %all-gather.4.cloned.1.call-start = ((), (), s32[]{:S(2)}) async-start(), calls=%async_computation | async-start | bytes 1114112 | tf_op jit(solution)/shard_map/all_gather | solution.py:114
  8.6 393.1 %all-gather.8.cloned.1.call-start = ((), (), s32[]{:S(2)}) async-start(), calls=%async_computation.2 | async-start | bytes 1114112 | tf_op jit(solution)/shard_map/all_gather | solution.py:133
  94.8 4.0 copy-start
  166.7 2.6 copy-start.1
Sparse Core Ops, SparseCore 0:
  11.3 83.4 all-gather.5
  98.1 68.5 all-gather.3
  315.9 85.7 all-gather.7
where the time goes:
time: 503 us; the launch traced here: 501 us
  waiting for transfers between devices  235 us (47%)
  other arithmetic  114 us (23%)
  blocking collectives  102 us (20%)
  matrix products  25.9 us (5%)
  between operations  13.9 us (3%)
  local copies, waits for them, and re-layouts  6.49 us (1%)
    psum x1, blocking collectives, local(): lax.psum((jnp.sum(mixed * mixed, axis=1), jnp.sum(upstream * mixed, axis=...  102 us
    all_gather x1, waiting for transfers between devices, local(): all_inner = lax.all_gather(d_inner, 'ctx', axis=0, tiled=True)  84.4 us
    all_gather x1, waiting for transfers between devices, local(): all_inputs = lax.all_gather(inputs, 'ctx', axis=0, tiled=True)  84.2 us
    all_gather x1, waiting for transfers between devices, local(): all_taps = lax.all_gather(filter_taps, 'ctx', axis=0, tiled=True)  65.2 us
    scatter-add x32, other arithmetic, owner_advance(): imags = imags.at[target].add(addend[1])  39.1 us
    scatter-add x32, other arithmetic, backward_advance(): imags = imags.at[target].add(addend[1])  37.3 us
    scatter-add x32, other arithmetic, forward_advance(): imags = imags.at[target].add(addend[1])  37.3 us
  transfers between devices with their start and end apart: 3, of which 3 were waited for; matrix products, arithmetic and copies ran while one was open for 2% of the time, Pallas kernels for 0%

commit v1 on v0

--- a/solution.py
+++ b/solution.py
@@ -113,7 +113,9 @@
     fwd_cos, fwd_sin, inv_cos, inv_sin = tables(block_len)
     all_taps = lax.all_gather(filter_taps, "ctx", axis=0, tiled=True)
     taps_spec = spectrum(all_taps, block_len, fwd_cos, fwd_sin)
-    all_inputs = lax.all_gather(inputs, "ctx", axis=0, tiled=True)
+    all_inputs = jnp.concatenate(
+        lax.all_to_all(jnp.stack([inputs] * lax.axis_size("ctx")), "ctx", 0, 0), axis=0
+    )
     input_spec = spectrum(all_inputs, block_len, fwd_cos, fwd_sin)
     conv_real, conv_imag = forward_terms(taps_spec, input_spec, first_block, slot_count + 1)
     waves = inverse_many(conv_real, conv_imag, inv_cos, inv_sin)

time: 503 us -> 477 us (0.948)
  waiting for transfers between devices: 235 us -> 191 us
  starting transfers between devices: 0.11 us -> 19.1 us
    all_gather x1 -> x0, waiting for transfers between devices: 84.2 us -> none  [local(): all_inputs = lax.all_gather(inputs, 'ctx', axis=0, tiled=True)]
    all_gather x1, waiting for transfers between devices: 65.2 us -> 106 us  [local(): all_taps = lax.all_gather(filter_taps, 'ctx', axis=0, tiled=True)]
    all_to_all x0 -> x1, starting transfers between devices: none -> 19.1 us  [local(): lax.all_to_all(jnp.stack([inputs] * lax.axis_size('ctx')), 'ctx', 0, 0)]
  transfers between devices with their start and end apart: 3 -> 3, of which waited for: 3 -> 2; matrix products, arithmetic and copies ran while one was open for 2% -> 1% of each run, Pallas kernels for 0% -> 0%
where the time goes in v1:
time: 477 us; the launch traced here: 475 us
  waiting for transfers between devices  191 us (40%)
  other arithmetic  114 us (24%)
  blocking collectives  102 us (21%)
  matrix products  24.6 us (5%)
  starting transfers between devices  19.1 us (4%)
  between operations  14.2 us (3%)
  local copies, waits for them, and re-layouts  6.76 us (1%)
    all_gather x1, waiting for transfers between devices, local(): all_taps = lax.all_gather(filter_taps, 'ctx', axis=0, tiled=True)  106 us
    psum x1, blocking collectives, local(): lax.psum((jnp.sum(mixed * mixed, axis=1), jnp.sum(upstream * mixed, axis=...  102 us
    all_gather x1, waiting for transfers between devices, local(): all_inner = lax.all_gather(d_inner, 'ctx', axis=0, tiled=True)  84.4 us
    scatter-add x32, other arithmetic, owner_advance(): imags = imags.at[target].add(addend[1])  39.1 us
    scatter-add x32, other arithmetic, forward_advance(): imags = imags.at[target].add(addend[1])  37.3 us
    scatter-add x32, other arithmetic, backward_advance(): imags = imags.at[target].add(addend[1])  37.3 us
    all_to_all x1, starting transfers between devices, local(): lax.all_to_all(jnp.stack([inputs] * lax.axis_size('ctx')), 'ctx', 0, 0)  19.1 us
  transfers between devices with their start and end apart: 3, of which 2 were waited for; matrix products, arithmetic and copies ran while one was open for 1% of the time, Pallas kernels for 0%

profile of v1, /device:TPU:1, one launch (start us, length us, event | category | flops | bytes accessed | tf_op | source)
XLA Modules:
  0.0 475.1 jit_solution(2738865523812884529)
XLA Ops:
  7.2 2.0 stack.2
  9.1 19.1 %all-to-all-start = ((bf16[16,128,256]{2,1,0:T(8,128)(2,1)}), bf16[16,128,256]{2,1,0:T(8,128)(2,1)S(1)}, u32[]{:S(2)}, u32[]{:S(2)}) async-start(bf16[16,128,256]{2,1,0:T(8,128)(2,1)} %stack.2), calls=%async_computation | async-start | bytes 2097152 | tf_op jit(solution)/shard_map/all_to_all | solution.py:117
  29.3 106.3 %all-gather.3.cloned.1.call-done = bf16[2048,256]{1,0:T(8,128)(2,1)} async-done(((bf16[128,256]{1,0:T(8,128)(2,1)}), bf16[2048,256]{1,0:T(8,128)(2,1)}) %all-gather.3.cloned.1.call-update) | async-done | bytes 1048592 | tf_op jit(solution)/shard_map/all_gather | solution.py:114
  135.5 2.6 convolution_bitcast_fusion.2
  138.1 2.6 negate_bitcast_fusion.2
  140.7 2.7 convolution_bitcast_fusion.1
  143.5 2.6 negate_bitcast_fusion.1
  146.1 38.1 %while.63 = (s32[]{:T(128)}, f32[2,129,256]{2,1,0:T(8,128)S(1)}, f32[2,129,256]{2,1,0:T(8,128)S(1)}, f32[16,129,256]{2,1,0:T(8,128)S(1)}, s32[]{:T(128)}, /*inde...) while((s32[]{:T(128)}, f32[2,129,256]{2,1,0:T(8,128)S(1)}, ...), condition=%wide.region_1.2_spmd, body=%wide.region_0.1_spmd.sunk | while | flops 792593 | bytes 2185508 | solution.py:74
  184.2 1.4 fusion.19
  185.7 1.5 fusion.8
  187.2 102.0 %all-reduce = (f32[128]{0:T(128)S(1)}, f32[128]{0:T(128)S(1)}) all-reduce(f32[128]{0:T(128)S(1)} %get-tuple-element.897, f32[128]{0:T(128)S(1)} %get-tuple-element.896), channel_id=1, replica_groups=mesh['chan'=32,'ctx'=16] {'chan'}, use_global_device_ids=true, to_apply=%region_3.4 | all-reduce | flops 256 | bytes 2048 | tf_op jit(solution)/shard_map/psum | solution.py:126
  291.4 84.4 %all-gather.5.cloned.1.call-done = bf16[2048,256]{0,1:T(8,128)(2,1)} async-done(((bf16[128,256]{0,1:T(8,128)(2,1)}), bf16[2048,256]{0,1:T(8,128)(2,1)}) %all-gather.5.cloned.1.call-update) | async-done | bytes 1048592 | tf_op jit(solution)/shard_map/all_gather | solution.py:135
  375.9 1.5 copy.16
  377.4 2.6 convolution_bitcast_fusion
  380.0 2.7 negate_bitcast_fusion
  382.7 40.0 %while.65 = (s32[]{:T(128)}, f32[2,129,256]{2,1,0:T(8,128)S(1)}, f32[2,129,256]{2,1,0:T(8,128)S(1)}, s32[]{:T(128)}, f32[16,129,256]{2,1,0:T(8,128)}, /*index=5*...) while((s32[]{:T(128)}, f32[2,129,256]{2,1,0:T(8,128)S(1)}, ...), condition=%wide.region_9.10_spmd, body=%wide.region_8.9_spmd.sunk | while | flops 792593 | bytes 2171172 | solution.py:104
  384.0 1.2 fusion.131
  386.5 1.2 fusion.131
  389.0 1.2 fusion.131
  422.7 1.4 fusion.15
  424.2 1.5 fusion.6
  426.5 38.1 %while.64 = (s32[]{:T(128)}, f32[2,129,256]{2,1,0:T(8,128)S(1)}, f32[2,129,256]{2,1,0:T(8,128)S(1)}, f32[16,129,256]{2,1,0:T(8,128)S(1)}, s32[]{:T(128)}, /*inde...) while((s32[]{:T(128)}, f32[2,129,256]{2,1,0:T(8,128)S(1)}, ...), condition=%wide.region_7.8_spmd, body=%wide.region_6.7_spmd.sunk | while | flops 792593 | bytes 2185508 | solution.py:89
  464.6 1.4 fusion.17
  466.0 1.5 fusion.7
  (122 shorter events, 114.9 us)
Async XLA Ops:
  7.2 21.8 %copy-start.1 = (bf16[128,256]{1,0:T(8,128)(2,1)S(1)}, bf16[128,256]{1,0:T(8,128)(2,1)}, u32[]{:S(2)}) copy-start(bf16[128,256]{1,0:T(8,128)(2,1)} %param.35) | copy-start | bytes 196612
  7.2 21.9 %copy-start.2 = (bf16[128,256]{1,0:T(8,128)(2,1)S(1)}, bf16[128,256]{1,0:T(8,128)(2,1)}, u32[]{:S(2)}) copy-start(bf16[128,256]{1,0:T(8,128)(2,1)} %param.37) | copy-start | bytes 196612
  9.1 131.6 %all-to-all-start = ((bf16[16,128,256]{2,1,0:T(8,128)(2,1)}), bf16[16,128,256]{2,1,0:T(8,128)(2,1)S(1)}, u32[]{:S(2)}, u32[]{:S(2)}) async-start(bf16[16,128,256]{2,1,0:T(8,128)(2,1)} %stack.2), calls=%async_computation | async-start | bytes 2097152 | tf_op jit(solution)/shard_map/all_to_all | solution.py:117
  28.2 107.3 %all-gather.3.cloned.1.call-start = ((), (), s32[]{:S(2)}) async-start(), calls=%async_computation.1 | async-start | bytes 1114112 | tf_op jit(solution)/shard_map/all_gather | solution.py:114
  28.9 347.0 %all-gather.5.cloned.1.call-start = ((), (), s32[]{:S(2)}) async-start(), calls=%async_computation.2 | async-start | bytes 1114112 | tf_op jit(solution)/shard_map/all_gather | solution.py:135
  135.5 2.6 copy-start
Sparse Core Ops, SparseCore 0:
  32.4 103.1 all-gather.2
  290.1 85.7 all-gather.4
